TPU v7x, 128 devices: a whole 4x4x4 slice. The times are simulated.
128 devices in a mesh: front: 8 (over y, core), blk: 16 (over z, x).
Axes of the slice: x: 4, y: 4, z: 4, core: 2. Of those that a mesh axis runs over, the one named last changes fastest.
Arguments:
- front: float32 [49152, 6144], P('front', 'blk'), may hold values from -8 to 96, as said below
- parent_group: int32 [8, 16, 6, 1], P('front', 'blk'), may hold values from 0 to 7; in each aligned block of 6 rows (0 to 5, 6 to 11, ..., all dimensions but the last counted through in order) at most 2 rows name the same one
- row_block: int32 [8, 16, 6], P('front', 'blk'), may hold values from 0 to 7
- parent_base: float32 [8192, 6144], P('front', 'blk'), may hold values from -6 to 6
Outputs:
- factored: float32 [49152, 6144], P('front', 'blk')
- assembled: float32 [8192, 6144], P('front', 'blk')
Inputs may be any that keep to these rules, and one draw needn't show every extreme that they name: `parent_group`: in the 6 blocks of one device no group is named more than 2 times. `front`: diagonal entries at indices pivotal at some tick lie between 48 and 96; every other entry lies within 8 of zero.
All inputs are finite; a program needn't handle non-finite values.
Results may differ from a plain program's by a relative error of at most 0.003.
Values may be sent and summed in bfloat16 or wider, within the bound.
A program may use at most 128 MiB of HBM per device.

v0:
```python
import jax
import jax.numpy as jnp
from jax import lax
from jax.sharding import PartitionSpec as P

P_SIZE = 256
TICKS = 5
NEWTON = 2
RB = 128
NB = 6
CAP = 2
ASM_BLOCKS = 8


def broadcast(value, axis, source):
    kept = jnp.where(lax.axis_index(axis) == source, value, 0).astype(value.dtype)
    return lax.psum(kept, axis)


def newton_inverse(block):
    inverse = jnp.diag(1.0 / jnp.diagonal(block))
    ident = jnp.eye(block.shape[0], dtype=block.dtype)
    for step in range(NEWTON):
        inverse = jnp.dot(
            inverse,
            2.0 * ident - jnp.dot(block, inverse, precision=lax.Precision.HIGHEST),
            precision=lax.Precision.HIGHEST,
        )
    return inverse


def local(front, parent_group, row_block, parent_base):
    order, width = front.shape
    member = lax.axis_index("blk")
    groups = lax.axis_size("front")
    index = jnp.arange(order)
    pivotal = index % width < P_SIZE
    left = front[:, :P_SIZE]
    right = front[:, P_SIZE:]
    for tick in range(TICKS):
        start = tick * width
        factor_left = left
        factor_start = tick * width
        live = jnp.logical_not(pivotal & (index // width <= tick))

        def owner_part(cols):
            inverse = newton_inverse(cols[factor_start : factor_start + P_SIZE, :])
            mult = jnp.dot(cols, inverse, precision=lax.Precision.HIGHEST)
            return mult * live[:, None].astype(cols.dtype)

        def other_part(cols):
            return jnp.zeros_like(cols)

        mult = lax.cond(member == tick, owner_part, other_part, factor_left)
        panel = broadcast(mult.astype(jnp.bfloat16), "blk", tick)
        factor_left = jnp.where((member == tick) & live[:, None], mult, factor_left)
        panel, left = (panel, factor_left)
        urows_left = left[start : start + P_SIZE, :].astype(jnp.bfloat16)
        urows_right = right[start : start + P_SIZE, :].astype(jnp.bfloat16)
        left_mask = (member > tick).astype(jnp.float32)
        left = left - jnp.dot(panel, urows_left, preferred_element_type=jnp.float32) * left_mask
        right = right - jnp.dot(panel, urows_right, preferred_element_type=jnp.float32)
    factored = jnp.concatenate([left, right], axis=1)
    tail_rows = order - NB * RB
    keep_left = (member >= TICKS).astype(jnp.float32)
    tail = jnp.concatenate([left[tail_rows:, :] * keep_left, right[tail_rows:, :]], axis=1)
    cont = tail.astype(jnp.bfloat16).reshape(NB, RB, width)
    dest = parent_group.reshape(NB)
    target_block = row_block.reshape(NB)
    offset_hot = (target_block[:, None] == jnp.arange(ASM_BLOCKS, dtype=jnp.int32)[None, :]).astype(
        jnp.bfloat16
    )
    number = jnp.arange(NB)
    earlier = (dest[None, :] == dest[:, None]) & (number[None, :] < number[:, None])
    slot = jnp.sum(earlier.astype(jnp.int32), axis=1)
    pick = (dest[None, None, :] == jnp.arange(groups, dtype=jnp.int32)[:, None, None]) & (
        slot[None, None, :] == jnp.arange(CAP, dtype=jnp.int32)[None, :, None]
    )
    pick = pick.astype(jnp.bfloat16)
    outgoing = jnp.einsum("gci,irk->gcrk", pick, cont, preferred_element_type=jnp.float32).astype(
        jnp.bfloat16
    )
    address = jnp.einsum(
        "gci,ia->gca", pick, offset_hot, preferred_element_type=jnp.float32
    ).astype(jnp.bfloat16)
    incoming, received_address = (
        lax.all_to_all(outgoing, "front", split_axis=0, concat_axis=0, tiled=True),
        lax.all_to_all(address, "front", split_axis=0, concat_axis=0, tiled=True),
    )
    added = jnp.einsum(
        "gca,gcrk->ark", received_address, incoming, preferred_element_type=jnp.float32
    )
    assembled = parent_base + added.reshape(ASM_BLOCKS * RB, width)
    return (factored, assembled)


def solution(mesh):
    placed = (
        P("front", "blk"),
        P("front", "blk", None, None),
        P("front", "blk", None),
        P("front", "blk"),
    )
    return jax.shard_map(
        local,
        mesh=mesh,
        in_specs=placed,
        out_specs=(P("front", "blk"), P("front", "blk")),
        check_vma=False,
    )
```

profile of v0, /device:TPU:4, one launch (start us, length us, event | category | flops | bytes accessed | tf_op | source)
XLA Modules:
  0.0 708.6 jit_solution(14253200812912760394)
XLA Ops:
  7.3 5.9 slice.69
  13.2 3.4 conditional.5
  13.2 3.4 broadcast.300
  16.6 4.8 convert_select_fusion.4
  21.4 6.6 copy.29
  28.0 8.2 %broadcast_select_fusion = f32[6144,256]{1,0:T(8,128)} fusion(f32[6144,256]{1,0:T(8,128)} %copy.29, pred[6144]{0:T(1024)(128)(4,1)S(1)} %not_and_fusion, f32[6144,384]{1,0:T(8,128)} %param.14), kind=kLoop, calls=%fused_computation.131 | loop fusion | flops 1572864 | bytes 18880512 | tf_op jit(solution)/shard_map/jit(_where)/select_n | solution.py:56
  36.2 98.2 %all-reduce.6.cloned.1.call-done = bf16[6144,256]{0,1:T(8,128)(2,1)} async-done(((bf16[6144,256]{0,1:T(8,128)(2,1)}), bf16[6144,256]{0,1:T(8,128)(2,1)}) %all-reduce.6.cloned.1.call-update) | async-done | bytes 3145744 | tf_op jit(solution)/shard_map/psum | solution.py:17
  134.4 7.6 %fusion.74 = f32[6144,256]{1,0:T(8,128)} fusion(f32[6144,256]{1,0:T(8,128)} %broadcast_select_fusion, bf16[6144,256]{0,1:T(8,128)(2,1)} %all-reduce.6.cloned.1.call-done, f32[]{:T(128)S(6)} %convert_element_type.108), kind=kOutput, calls=%fused_computation.120 | convolution fusion | flops 808517632 | bytes 15990788 | tf_op jit(solution)/shard_map/dot_general | solution.py:61
  142.0 3.6 conditional.6
  142.0 3.4 broadcast.303
  145.6 4.8 convert_select_fusion.3
  150.5 6.6 copy.30
  157.1 8.2 %broadcast_select_fusion.1 = f32[6144,256]{1,0:T(8,128)} fusion(f32[6144,256]{1,0:T(8,128)} %copy.30, f32[6144,256]{1,0:T(8,128)} %fusion.74, pred[6144]{0:T(1024)(128)(4,1)S(1)} %not_and_fusion.1), kind=kLoop, calls=%fused_computation.132 | loop fusion | flops 1572864 | bytes 18880512 | tf_op jit(solution)/shard_map/jit(_where)/select_n | solution.py:56
  165.2 99.2 %all-reduce.8.cloned.1.call-done = bf16[6144,256]{0,1:T(8,128)(2,1)} async-done(((bf16[6144,256]{0,1:T(8,128)(2,1)}), bf16[6144,256]{0,1:T(8,128)(2,1)}) %all-reduce.8.cloned.1.call-update) | async-done | bytes 3145744 | tf_op jit(solution)/shard_map/psum | solution.py:17
  264.4 7.6 %fusion.73 = f32[6144,256]{1,0:T(8,128)} fusion(f32[6144,256]{1,0:T(8,128)} %broadcast_select_fusion.1, bf16[6144,256]{0,1:T(8,128)(2,1)} %all-reduce.8.cloned.1.call-done, f32[]{:T(128)S(6)} %convert_element_type.110), kind=kOutput, calls=%fused_computation.118 | convolution fusion | flops 808517632 | bytes 15990788 | tf_op jit(solution)/shard_map/dot_general | solution.py:61
  272.0 25.5 %conditional.7 = (f32[6144,256]{0,1:T(8,128)}) conditional(s32[]{:T(128)} %convert_element_type.104, () %tuple.40, (f32[6144,256]{1,0:T(8,128)}, s32[6144]{0:T(1024)S(1)}, pred[6144]{0:T(1024)(128)(4,1)S(1)}) %tuple.45), branch_computations={%region_6.7_spmd, %region_7.8_spmd} | conditional | flops 5639398400 | bytes 16079880 | solution.py:54
  273.3 2.3 gather_fusion.2
  279.5 18.0 %fusion.28 = f32[6144,256]{0,1:T(8,128)} fusion(f32[256,256]{1,0:T(8,128)S(1)} %fusion.104, f32[6144,256]{1,0:T(8,128)} %get-tuple-element.76, f32[6144]{0:T(1024)S(1)} %not_convert_fusion.2), kind=kOutput, calls=%fused_computation.48 | convolution fusion | flops 4833411072 | bytes 12869632 | tf_op jit(solution)/shard_map/cond/branch_1_fun/dot_general | solution.py:48
  297.5 4.8 convert_select_fusion.2
  302.3 6.6 copy.31
  308.9 8.5 %broadcast_select_fusion.2 = f32[6144,256]{1,0:T(8,128)} fusion(f32[6144,256]{1,0:T(8,128)} %copy.31, f32[6144,256]{1,0:T(8,128)} %fusion.73, pred[6144]{0:T(1024)(128)(4,1)S(1)} %not_and_fusion.2), kind=kLoop, calls=%fused_computation.133 | loop fusion | flops 1572864 | bytes 18880512 | tf_op jit(solution)/shard_map/jit(_where)/select_n | solution.py:56
  317.4 78.5 %all-reduce.10.cloned.1.call-done = bf16[6144,256]{0,1:T(8,128)(2,1)} async-done(((bf16[6144,256]{0,1:T(8,128)(2,1)}), bf16[6144,256]{0,1:T(8,128)(2,1)}) %all-reduce.10.cloned.1.call-update) | async-done | bytes 3145744 | tf_op jit(solution)/shard_map/psum | solution.py:17
  395.9 7.6 %fusion.72 = f32[6144,256]{1,0:T(8,128)} fusion(f32[6144,256]{1,0:T(8,128)} %broadcast_select_fusion.2, bf16[6144,256]{0,1:T(8,128)(2,1)} %all-reduce.10.cloned.1.call-done, f32[]{:T(128)S(6)} %convert_element_type.112), kind=kOutput, calls=%fused_computation.116 | convolution fusion | flops 808517632 | bytes 15990788 | tf_op jit(solution)/shard_map/dot_general | solution.py:61
  403.4 3.6 conditional.8
  403.4 3.4 broadcast.309
  407.1 4.8 convert_select_fusion.1
  412.9 4.3 all-to-all-start
  417.3 6.6 copy.32
  423.9 8.2 %broadcast_select_fusion.3 = f32[6144,256]{1,0:T(8,128)} fusion(f32[6144,256]{1,0:T(8,128)} %copy.32, f32[6144,256]{1,0:T(8,128)} %fusion.72, pred[6144]{0:T(1024)(128)(4,1)S(1)} %not_and_fusion.3), kind=kLoop, calls=%fused_computation.134 | loop fusion | flops 1572864 | bytes 18880512 | tf_op jit(solution)/shard_map/jit(_where)/select_n | solution.py:56
  432.0 95.1 %all-reduce.12.cloned.1.call-done = bf16[6144,256]{0,1:T(8,128)(2,1)} async-done(((bf16[6144,256]{0,1:T(8,128)(2,1)}), bf16[6144,256]{0,1:T(8,128)(2,1)}) %all-reduce.12.cloned.1.call-update) | async-done | bytes 3145744 | tf_op jit(solution)/shard_map/psum | solution.py:17
  527.1 7.6 %fusion.71 = f32[6144,256]{1,0:T(8,128)} fusion(f32[6144,256]{1,0:T(8,128)} %broadcast_select_fusion.3, bf16[6144,256]{0,1:T(8,128)(2,1)} %all-reduce.12.cloned.1.call-done, f32[]{:T(128)S(6)} %convert_element_type.114), kind=kOutput, calls=%fused_computation.114 | convolution fusion | flops 808517632 | bytes 15990788 | tf_op jit(solution)/shard_map/dot_general | solution.py:61
  534.7 12.3 %conditional.9 = (f32[6144,256]{0,1:T(8,128)}) conditional(s32[]{:T(128)} %convert_element_type.102, () %tuple.38, (f32[6144,256]{1,0:T(8,128)}, s32[6144]{0:T(1024)S(1)}, pred[6144]{0:T(1024)(128)(4,1)S(1)}) %tuple.47), branch_computations={%region_12.13_spmd, %region_13.14_spmd} | conditional | flops 5639398400 | bytes 16079880 | solution.py:54
  534.7 3.4 broadcast.312
  547.0 5.0 convert_select_fusion
  552.0 3.1 convolution_subtract_fusion.4
  557.0 2.7 convolution_subtract_fusion.2
  559.7 6.7 copy.33
  566.4 4.8 convolution_subtract_fusion.1
  571.2 6.9 broadcast_select_fusion.4
  578.1 79.4 %all-reduce.14.cloned.1.call-done = bf16[6144,256]{0,1:T(8,128)(2,1)} async-done(((bf16[6144,256]{0,1:T(8,128)(2,1)}), bf16[6144,256]{0,1:T(8,128)(2,1)}) %all-reduce.14.cloned.1.call-update) | async-done | bytes 3145744 | tf_op jit(solution)/shard_map/psum | solution.py:17
  657.5 4.1 convolution_subtract_fusion
  661.8 4.0 fusion.70
  665.7 2.7 copy-done
  669.3 2.4 copy.37
  671.6 4.3 all-to-all-start.1
  676.0 7.1 %pad_maximum_fusion = f32[6144,384]{1,0:T(8,128)} fusion(f32[6144,128]{1,0:T(8,128)S(1)} %convolution_subtract_fusion, f32[6144,256]{1,0:T(8,128)} %copy-done), kind=kLoop, calls=%fused_computation.110 | loop fusion | flops 2359296 | bytes 18874368 | tf_op jit(solution)/shard_map/concatenate | solution.py:63
  683.1 14.5 %all-to-all-done.1 = bf16[8,2,128,384]{3,1,2,0:T(2,128)(2,1)} async-done(((bf16[8,2,128,384]{3,1,2,0:T(2,128)(2,1)}), bf16[8,2,128,384]{3,1,2,0:T(2,128)(2,1)}, u32[]{:S(2)}, u32[]{:S(2)}) %all-to-all-start.1) | async-done | bytes 1572896 | tf_op jit(solution)/shard_map/all_to_all | solution.py:87
  697.6 2.4 fusion.77
  (59 shorter events, 10.8 us)
Async XLA Ops:
  7.2 127.3 %all-reduce.6.cloned.1.call-start = ((), (), s32[]{:S(2)}) async-start(), calls=%async_computation.2 | async-start | bytes 6291456 | tf_op jit(solution)/shard_map/psum | solution.py:17
  21.4 243.0 %all-reduce.8.cloned.1.call-start = ((), (), s32[]{:S(2)}) async-start(), calls=%async_computation.3 | async-start | bytes 6291456 | tf_op jit(solution)/shard_map/psum | solution.py:17
  150.4 245.4 %all-reduce.10.cloned.1.call-start = ((), (), s32[]{:S(2)}) async-start(), calls=%async_computation.4 | async-start | bytes 6291456 | tf_op jit(solution)/shard_map/psum | solution.py:17
  302.2 224.8 %all-reduce.12.cloned.1.call-start = ((), (), s32[]{:S(2)}) async-start(), calls=%async_computation.5 | async-start | bytes 6291456 | tf_op jit(solution)/shard_map/psum | solution.py:17
  407.0 4.8 copy-start.8
  407.1 5.0 copy-start.9
  412.9 258.7 %all-to-all-start = ((bf16[8,2,8]{2,1,0:T(2,128)(2,1)}), bf16[8,2,8]{2,1,0:T(2,128)(2,1)S(1)}, u32[]{:S(2)}, u32[]{:S(2)}) async-start(bf16[8,2,8]{2,1,0:T(2,128)(2,1)} %copy.34), calls=%async_computation | async-start | bytes 8192 | tf_op jit(solution)/shard_map/all_to_all | solution.py:88
  417.2 240.3 %all-reduce.14.cloned.1.call-start = ((), (), s32[]{:S(2)}) async-start(), calls=%async_computation.6 | async-start | bytes 6291456 | tf_op jit(solution)/shard_map/psum | solution.py:17
  546.9 5.0 copy-start.1
  552.0 3.2 copy-start.2
  555.1 1.9 copy-start.3
  559.7 6.7 copy-start.4
  566.4 4.8 copy-start.6
  657.5 4.3 copy-start.5
  665.7 2.7 copy-start
  671.6 26.0 %all-to-all-start.1 = ((bf16[8,2,128,384]{3,1,2,0:T(2,128)(2,1)}), bf16[8,2,128,384]{3,1,2,0:T(2,128)(2,1)}, u32[]{:S(2)}, u32[]{:S(2)}) async-start(bf16[8,2,128,384]{3,1,2,0:T(2,128)(2,1)} %copy.37), calls=%async_computation.1 | async-start | bytes 3145728 | tf_op jit(solution)/shard_map/all_to_all | solution.py:87
  683.1 17.1 %copy-start.7 = (f32[1024,384]{1,0:T(8,128)S(1)}, f32[1024,384]{1,0:T(8,128)}, u32[]{:S(2)}) copy-start(f32[1024,384]{1,0:T(8,128)} %param.17) | copy-start | bytes 4718596
Sparse Core Ops, SparseCore 0:
  21.5 112.8 all-reduce.5
  150.6 113.7 all-reduce.7
  302.4 93.4 all-reduce.9
  412.0 115.0 all-reduce.11
  552.1 105.3 all-reduce.13
where the time goes:
time: 720 us; the launch traced here: 709 us
  waiting for transfers between devices  465 us (65%)
  matrix products  74.8 us (10%)
  other arithmetic  72.8 us (10%)
  local copies, waits for them, and re-layouts  63.1 us (9%)
  between operations  14.5 us (2%)
  loops' own time  9.64 us (1%)
  starting transfers between devices  8.78 us (1%)
    psum x5, waiting for transfers between devices, broadcast(): return lax.psum(kept, axis)  450 us
    select_n x5, other arithmetic, local(): factor_left = jnp.where((member == tick) & live[:, None], mult, factor_left)  39.8 us
    dot_general x5, matrix products, local(): jnp.dot(panel, urows_left, preferred_element_type=jnp.float32) * left_mask  34.2 us
    cond x5, local copies, waits for them, and re-layouts, local(): mult = lax.cond(member == tick, owner_part, other_part, factor_left)  32.9 us
    select_n x5, other arithmetic, broadcast(): jnp.where(lax.axis_index(axis) == source, value, 0).astype(value.dtype)  24.1 us
    dot_general x1, matrix products, owner_part(): mult = jnp.dot(cols, inverse, precision=lax.Precision.HIGHEST)  18 us
    dot_general x5, matrix products, local(): jnp.dot(panel, urows_right, preferred_element_type=jnp.float32)  15.7 us
    all_to_all x1, waiting for transfers between devices, local(): lax.all_to_all(outgoing, 'front', split_axis=0, concat_axis=0, tiled=True)  14.5 us
  transfers between devices with their start and end apart: 7, of which 6 were waited for; matrix products, arithmetic and copies ran while one was open for 17% of the time, Pallas kernels for 0%

commit v1 on v0

v1 whole, which is shorter than its diff:
```python
import jax
import jax.numpy as jnp
from jax import lax
from jax.experimental import pallas as pl
from jax.experimental.pallas import tpu as pltpu
from jax.sharding import PartitionSpec as P

P_SIZE = 256
TICKS = 5
RB = 128
NB = 6
CAP = 2
ASM_BLOCKS = 8
SIDE = 4
WIDTH = 384
BLOCK = 256
HALF = BLOCK // 2
BLOCKS = 24
F32 = jnp.float32
BF16 = jnp.bfloat16

STEPS = ((1, 0), (0, 1), (-1, 0), (0, -1))
PARENT = {
    (1, 0): 0, (2, 0): 0, (3, 0): 0, (0, 1): 2, (1, 1): 1, (2, 1): 0, (3, 1): 0, (0, 2): 2,
    (1, 2): 1, (2, 2): 1, (3, 2): 0, (0, 3): 2, (1, 3): 3, (2, 3): 3, (3, 3): 0,
}
SENDERS = tuple(
    sorted(
        ((x - STEPS[way][0]) % SIDE) + SIDE * ((z - STEPS[way][1]) % SIDE)
        for (x, z), own in PARENT.items()
        if own == way
    )
    for way in range(4)
)


def pieces(block):
    if block < TICKS:
        return ((block * WIDTH, BLOCK),)
    if block < 8:
        return ((5376 + (block - TICKS) * BLOCK, BLOCK),)
    if block < 10:
        first = (block - 8) * 2 * WIDTH + P_SIZE
        return ((first, HALF), (first + WIDTH, HALF))
    return ((1792 + (block - 10) * BLOCK, BLOCK),)


def split(value):
    high = value.astype(BF16)
    return high, (value - high.astype(F32)).astype(BF16)


def dot(a, b):
    return jnp.dot(a, b, preferred_element_type=F32)


def dot3(a, b):
    return dot(a[0], b[0]) + dot(a[0], b[1]) + dot(a[1], b[0])


def kernel(front, out, rows, panel, urows, inv_high, inv_low, load_sem, store_sem, send_sem, recv_sem):
    me = lax.axis_index("blk")
    x = lax.rem(me, SIDE)
    z = lax.div(me, SIDE)
    around = [
        z * SIDE + lax.rem(x + 1, SIDE),
        lax.rem(z + 1, SIDE) * SIDE + x,
        z * SIDE + lax.rem(x + SIDE - 1, SIDE),
        lax.rem(z + SIDE - 1, SIDE) * SIDE + x,
    ]

    for block in range(BLOCKS):
        at = 0
        for start, size in pieces(block):
            pltpu.make_async_copy(
                front.at[pl.ds(start, size)], rows.at[block, pl.ds(at, size)], load_sem.at[block]
            ).start()
            at += size

    barrier = pltpu.get_barrier_semaphore()
    for other in around:
        pl.semaphore_signal(barrier, inc=1, device_id={"blk": other}, device_id_type=pl.DeviceIdType.MESH)
    pl.semaphore_wait(barrier, 4)

    def children(tick):
        dx = lax.rem(x - tick % SIDE + SIDE, SIDE)
        dz = lax.rem(z - tick // SIDE + SIDE, SIDE)
        nx, nz = lax.rem(SIDE - dx, SIDE), lax.rem(SIDE - dz, SIDE)
        turned = (dx + SIDE * dz, dz + SIDE * nx, nx + SIDE * nz, nz + SIDE * dx)
        result = []
        for tree in range(4):
            ways = []
            for way in range(4):
                has = turned[tree] == SENDERS[(way - tree) % 4][0]
                for node in SENDERS[(way - tree) % 4][1:]:
                    has = has | (turned[tree] == node)
                ways.append(has)
            result.append(ways)
        return result

    sends = [children(tick) for tick in range(TICKS)]

    def chunk_copy(tick, block, half, way):
        chunk = panel.at[tick, block, pl.ds(half * HALF, HALF)]
        return pltpu.make_async_remote_copy(
            src_ref=chunk,
            dst_ref=chunk,
            send_sem=send_sem.at[tick, way],
            recv_sem=recv_sem.at[tick, block, half],
            device_id={"blk": around[way]},
            device_id_type=pl.DeviceIdType.MESH,
        )

    def send(tick, block, pair):
        for half in range(2):
            tree = pair * 2 + half
            for way in range(4):
                @pl.when(sends[tick][tree][way])
                def _():
                    chunk_copy(tick, block, half, way).start()

    def receive(tick, block, pair):
        for half in range(2):
            tree = pair * 2 + half
            chunk_copy(tick, block, half, 0).wait_recv()
            for way in range(4):
                @pl.when(sends[tick][tree][way])
                def _():
                    chunk_copy(tick, block, half, way).start()

    def wait_load(block):
        pltpu.make_async_copy(front.at[pl.ds(0, BLOCK)], rows.at[block], load_sem.at[block]).wait()

    def store(block):
        return pltpu.make_async_copy(rows.at[block], out.at[block], store_sem.at[block])

    def invert(tick):
        matrix = rows[tick, :, :P_SIZE]
        line = lax.broadcasted_iota(jnp.int32, (P_SIZE, P_SIZE), 0)
        column = lax.broadcasted_iota(jnp.int32, (P_SIZE, P_SIZE), 1)
        eye = line == column
        on_diagonal = jnp.where(eye, matrix, 0.0)
        by_row = 1.0 / jnp.sum(on_diagonal, axis=1, keepdims=True)
        by_column = 1.0 / jnp.sum(on_diagonal, axis=0, keepdims=True)
        first = jnp.where(eye, 2.0 * by_row, 0.0) - by_row * matrix * by_column
        first = split(first)
        residual = jnp.where(eye, 2.0, 0.0) - dot3(split(matrix), first)
        high, low = split(dot3(first, split(residual)))
        inv_high[...] = high
        inv_low[...] = low

    def multiply(tick, block):
        mult = dot3(split(rows[block, :, :P_SIZE]), (inv_high[...], inv_low[...]))
        rows[block, :, :P_SIZE] = mult
        panel[tick, block] = mult.astype(BF16)

    def pivot_rows(tick):
        keep = jnp.where(me > tick, 1.0, 0.0).astype(F32)
        urows[:, :P_SIZE] = (rows[tick, :, :P_SIZE] * keep).astype(BF16)
        urows[:, P_SIZE:] = rows[tick, :, P_SIZE:].astype(BF16)

    def paired(first, body):
        body(first, 0)
        count = BLOCKS - 1 - first

        def step(index, carry):
            body(first + 1 + 2 * index, 1)
            body(first + 2 + 2 * index, 0)
            return carry

        lax.fori_loop(0, count // 2, step, 0)
        if count % 2:
            body(BLOCKS - 1, 1)

    wait_load(0)
    store(0).start()

    @pl.when(me == 0)
    def _():
        invert(0)

        def own(block, pair):
            wait_load(block)
            multiply(0, block)
            send(0, block, pair)

        paired(1, own)

    for tick in range(TICKS):
        pivot_rows(tick)

        def visit(block, pair):
            @pl.when(me != tick)
            def _():
                receive(tick, block, pair)
                if tick == 0:
                    wait_load(block)

            rows[block] = rows[block] - dot(panel[tick, block], urows[...])
            if tick + 1 < TICKS:
                is_pivot = isinstance(block, int) and block == tick + 1
                if is_pivot:
                    store(block).start()

                @pl.when(me == tick + 1)
                def _():
                    if is_pivot:
                        invert(tick + 1)
                    else:
                        multiply(tick + 1, block)
                        send(tick + 1, block, 1 - pair)
            else:
                store(block).start()

        paired(tick + 1, visit)

    for tick in range(TICKS):
        number = BLOCKS - 1 - tick
        for pair, amount in enumerate((number - number // 2, number // 2)):
            for way in range(4):
                @pl.when(sends[tick][2 * pair][way] | sends[tick][2 * pair + 1][way])
                def _():
                    sent = panel.at[tick, pl.ds(0, amount), pl.ds(0, HALF)]
                    pltpu.make_async_remote_copy(
                        src_ref=sent,
                        dst_ref=sent,
                        send_sem=send_sem.at[tick, way],
                        recv_sem=recv_sem.at[tick, 0, 0],
                        device_id={"blk": around[way]},
                        device_id_type=pl.DeviceIdType.MESH,
                    ).wait_send()
    for block in range(BLOCKS):
        store(block).wait()


def factor(front):
    return pl.pallas_call(
        kernel,
        out_shape=jax.ShapeDtypeStruct((BLOCKS, BLOCK, WIDTH), F32),
        in_specs=[pl.BlockSpec(memory_space=pl.ANY)],
        out_specs=pl.BlockSpec(memory_space=pl.ANY),
        scratch_shapes=[
            pltpu.VMEM((BLOCKS, BLOCK, WIDTH), F32),
            pltpu.VMEM((TICKS, BLOCKS, BLOCK, P_SIZE), BF16),
            pltpu.VMEM((P_SIZE, WIDTH), BF16),
            pltpu.VMEM((P_SIZE, P_SIZE), BF16),
            pltpu.VMEM((P_SIZE, P_SIZE), BF16),
            pltpu.SemaphoreType.DMA((BLOCKS,)),
            pltpu.SemaphoreType.DMA((BLOCKS,)),
            pltpu.SemaphoreType.DMA((TICKS, 4)),
            pltpu.SemaphoreType.DMA((TICKS, BLOCKS, 2)),
        ],
        compiler_params=pltpu.CompilerParams(
            collective_id=0, has_side_effects=True, vmem_limit_bytes=50 * 1024 * 1024
        ),
        name="factor",
    )(front)


def local(front, parent_group, row_block, parent_base):
    order, width = front.shape
    member = lax.axis_index("blk")
    groups = lax.axis_size("front")
    held = factor(front)
    parts = []
    for block in range(BLOCKS):
        at = 0
        for start, size in pieces(block):
            parts.append((start, held[block, at : at + size]))
            at += size
    parts.sort(key=lambda part: part[0])
    factored = jnp.concatenate([part[1] for part in parts], axis=0)

    keep_left = (member >= TICKS).astype(F32)
    tail = held[TICKS : TICKS + 3].reshape(NB * RB, width)
    tail = jnp.concatenate([tail[:, :P_SIZE] * keep_left, tail[:, P_SIZE:]], axis=1)
    cont = tail.astype(BF16).reshape(NB, RB, width)
    dest = parent_group.reshape(NB)
    target_block = row_block.reshape(NB)
    offset_hot = (target_block[:, None] == jnp.arange(ASM_BLOCKS, dtype=jnp.int32)[None, :]).astype(BF16)
    number = jnp.arange(NB)
    earlier = (dest[None, :] == dest[:, None]) & (number[None, :] < number[:, None])
    slot = jnp.sum(earlier.astype(jnp.int32), axis=1)
    pick = (dest[None, None, :] == jnp.arange(groups, dtype=jnp.int32)[:, None, None]) & (
        slot[None, None, :] == jnp.arange(CAP, dtype=jnp.int32)[None, :, None]
    )
    pick = pick.astype(BF16)
    outgoing = jnp.einsum("gci,irk->gcrk", pick, cont, preferred_element_type=F32).astype(BF16)
    address = jnp.einsum("gci,ia->gca", pick, offset_hot, preferred_element_type=F32).astype(BF16)
    incoming, received_address = (
        lax.all_to_all(outgoing, "front", split_axis=0, concat_axis=0, tiled=True),
        lax.all_to_all(address, "front", split_axis=0, concat_axis=0, tiled=True),
    )
    added = jnp.einsum("gca,gcrk->ark", received_address, incoming, preferred_element_type=F32)
    assembled = parent_base + added.reshape(ASM_BLOCKS * RB, width)
    return (factored, assembled)


def solution(mesh):
    placed = (
        P("front", "blk"),
        P("front", "blk", None, None),
        P("front", "blk", None),
        P("front", "blk"),
    )
    return jax.shard_map(
        local,
        mesh=mesh,
        in_specs=placed,
        out_specs=(P("front", "blk"), P("front", "blk")),
        check_vma=False,
    )
```

time: 720 us -> 1670 us (2.32)
  Pallas kernels: 0 us -> 1590 us
  waiting for transfers between devices: 465 us -> 10.9 us
  matrix products: 74.8 us -> 2.36 us
  other arithmetic: 72.8 us -> 2.95 us
    pallas_call x0 -> x1, Pallas kernels: none -> 1590 us  [factor(): pl.pallas_call(kernel, out_shape=jax.ShapeDtypeStruct((BLOCKS, BLOCK, WID...]
    psum x5 -> x0, waiting for transfers between devices: 450 us -> none  [broadcast(): return lax.psum(kept, axis)]
    dot_general x17 -> x2, matrix products: 72.4 us -> 1.39 us  [the longest x1 0.84 us: local(): jnp.einsum('gci,ia->gca', pick, offset_hot, preferred_element_type=F32)]
    select_n x11 -> x0, other arithmetic: 64 us -> none  [the longest x5 39.8 us: local(): factor_left = jnp.where((member == tick) & live[:, None], mult, factor_left)]
    unnamed x20 -> x27, local copies, waits for them, and re-layouts: 3.53 us -> 43.7 us
    cond x5 -> x0, local copies, waits for them, and re-layouts: 32.9 us -> none  [local(): mult = lax.cond(member == tick, owner_part, other_part, factor_left)]
  transfers between devices with their start and end apart: 7 -> 2, of which waited for: 6 -> 1; matrix products, arithmetic and copies ran while one was open for 17% -> 3% of each run, Pallas kernels for 0% -> 95%
where the time goes in v1:
time: 1670 us
  Pallas kernels  1590 us (95%)
  local copies, waits for them, and re-layouts  50.5 us (3%)
    pallas_call x1, Pallas kernels, factor(): pl.pallas_call(kernel, out_shape=jax.ShapeDtypeStruct((BLOCKS, BLOCK, WID...  1590 us
    unnamed x27, local copies, waits for them, and re-layouts  43.7 us
  transfers between devices with their start and end apart: 2, of which 1 were waited for; matrix products, arithmetic and copies ran while one was open for 3% of the time, Pallas kernels for 95%

profile of v1, /device:TPU:4, one launch (start us, length us, event | category | flops | bytes accessed | tf_op | source)
XLA Modules:
  0.0 1667.7 jit_solution(9958650130096730402)
XLA Ops:
  0.6 0.7 iota_compare_fusion.2
  1.3 0.9 convert_reduce_fusion
  2.2 0.8 convolution_convert_fusion.1
  3.1 0.6 copy.19
  3.6 4.5 all-to-all-start
  8.1 1590.3 %factor.1 = f32[24,256,384]{2,1,0:T(8,128)} custom-call(f32[6144,384]{1,0:T(8,128)} %front.1), custom_call_target="tpu_custom_call" | custom-call | tf_op jit(solution)/shard_map/factor/pallas_call | solution.py:237
  1598.5 1.8 bitcast_dynamic-update-slice_fusion.21
  1600.2 1.3 slice.114
  1601.6 1.6 bitcast_dynamic-update-slice_fusion.25
  1603.2 1.8 bitcast_dynamic-update-slice_fusion.20
  1605.0 1.6 bitcast_dynamic-update-slice_fusion.24
  1606.6 1.8 bitcast_dynamic-update-slice_fusion.19
  1608.4 1.6 bitcast_dynamic-update-slice_fusion.23
  1610.0 1.8 bitcast_dynamic-update-slice_fusion.18
  1611.7 1.6 bitcast_dynamic-update-slice_fusion.22
  1613.4 1.8 bitcast_dynamic-update-slice_fusion.17
  1615.1 1.8 bitcast_dynamic-update-slice_fusion.16
  1616.9 1.8 bitcast_dynamic-update-slice_fusion.15
  1618.6 1.8 bitcast_dynamic-update-slice_fusion.14
  1620.4 1.8 bitcast_dynamic-update-slice_fusion.13
  1622.2 1.8 bitcast_dynamic-update-slice_fusion.12
  1623.9 1.8 bitcast_dynamic-update-slice_fusion.11
  1625.7 1.8 bitcast_dynamic-update-slice_fusion.10
  1627.5 1.8 bitcast_dynamic-update-slice_fusion.9
  1629.2 1.8 bitcast_dynamic-update-slice_fusion.8
  1631.0 1.8 bitcast_dynamic-update-slice_fusion.7
  1632.8 0.1 fusion.5
  1632.9 0.2 copy.20
  1633.1 0.1 copy.21
  1633.3 0.5 convolution_convert_fusion
  1633.8 0.0 copy-start
  1633.8 1.9 bitcast_dynamic-update-slice_fusion.6
  1635.7 2.4 copy.22
  1638.1 0.0 all-to-all-done
  1638.1 5.5 all-to-all-start.1
  1643.5 1.8 bitcast_dynamic-update-slice_fusion.5
  1645.3 1.8 bitcast_dynamic-update-slice_fusion.4
  1647.1 1.8 bitcast_dynamic-update-slice_fusion.3
  1648.8 1.8 bitcast_dynamic-update-slice_fusion.2
  1650.6 1.8 bitcast_dynamic-update-slice_fusion.1
  1652.4 1.8 bitcast_dynamic-update-slice_fusion
  1654.1 0.1 copy.23
  1654.2 10.9 all-to-all-done.1
  1665.1 1.0 fusion.2
  1666.1 0.3 copy.25
  1666.4 0.0 copy-done
  1666.4 1.3 bitcast_add_fusion
  (2 shorter events, 0.0 us)
Async XLA Ops:
  3.6 1634.4 %all-to-all-start = ((bf16[8,2,8]{2,1,0:T(2,128)(2,1)}), bf16[8,2,8]{2,1,0:T(2,128)(2,1)S(1)}, u32[]{:S(2)}, u32[]{:S(2)}) async-start(bf16[8,2,8]{2,1,0:T(2,128)(2,1)} %copy.19), calls=%async_computation | async-start | bytes 8192 | tf_op jit(solution)/shard_map/all_to_all | solution.py:292
  1633.8 32.6 %copy-start = (f32[1024,384]{1,0:T(8,128)S(1)}, f32[1024,384]{1,0:T(8,128)}, u32[]{:S(2)}) copy-start(f32[1024,384]{1,0:T(8,128)} %param.7) | copy-start | bytes 4718596
  1638.1 27.1 %all-to-all-start.1 = ((bf16[8,2,128,384]{3,1,2,0:T(2,128)(2,1)}), bf16[8,2,128,384]{3,1,2,0:T(2,128)(2,1)S(1)}, u32[]{:S(2)}, u32[]{:S(2)}) async-start(bf16[8,2,128,384]{3,1,2,0:T(2,128)(2,1)} %copy.22), calls=%async_computation.1 | async-start | bytes 3145728 | tf_op jit(solution)/shard_map/all_to_all | solution.py:291

commit v2 on v1

--- a/solution.py
+++ b/solution.py
@@ -15,6 +15,9 @@
 WIDTH = 384
 BLOCK = 256
 HALF = BLOCK // 2
+CHUNK = BLOCK // 4
+LAG = 3
+BEHIND = 5 * LAG
 BLOCKS = 24
 F32 = jnp.float32
 BF16 = jnp.bfloat16
@@ -34,6 +37,18 @@
 )
 
 
+def depth_of(node):
+    depth = 0
+    while node != (0, 0):
+        step = STEPS[PARENT[node]]
+        node = ((node[0] - step[0]) % SIDE, (node[1] - step[1]) % SIDE)
+        depth += 1
+    return depth
+
+
+DEPTH = {x + SIDE * z: depth_of((x, z)) for x, z in PARENT}
+
+
 def pieces(block):
     if block < TICKS:
         return ((block * WIDTH, BLOCK),)
@@ -43,6 +58,10 @@
         first = (block - 8) * 2 * WIDTH + P_SIZE
         return ((first, HALF), (first + WIDTH, HALF))
     return ((1792 + (block - 10) * BLOCK, BLOCK),)
+
+
+def number(tick):
+    return BLOCKS - 1 - tick
 
 
 def split(value):
@@ -82,12 +101,13 @@
         pl.semaphore_signal(barrier, inc=1, device_id={"blk": other}, device_id_type=pl.DeviceIdType.MESH)
     pl.semaphore_wait(barrier, 4)
 
-    def children(tick):
+    def place(tick):
         dx = lax.rem(x - tick % SIDE + SIDE, SIDE)
         dz = lax.rem(z - tick // SIDE + SIDE, SIDE)
         nx, nz = lax.rem(SIDE - dx, SIDE), lax.rem(SIDE - dz, SIDE)
         turned = (dx + SIDE * dz, dz + SIDE * nx, nx + SIDE * nz, nz + SIDE * dx)
         result = []
+        lags = []
         for tree in range(4):
             ways = []
             for way in range(4):
@@ -96,43 +116,57 @@
                     has = has | (turned[tree] == node)
                 ways.append(has)
             result.append(ways)
-        return result
-
-    sends = [children(tick) for tick in range(TICKS)]
-
-    def chunk_copy(tick, block, half, way):
-        chunk = panel.at[tick, block, pl.ds(half * HALF, HALF)]
+            lag = jnp.int32(0)
+            for node, depth in DEPTH.items():
+                lag = jnp.where(turned[tree] == node, depth * LAG, lag)
+            lags.append(lag)
+        return result, lags
+
+    places = [place(tick) for tick in range(TICKS)]
+
+    def chunk_copy(tick, block, tree, way):
+        chunk = panel.at[tick, block, pl.ds(tree * CHUNK, CHUNK)]
         return pltpu.make_async_remote_copy(
             src_ref=chunk,
             dst_ref=chunk,
             send_sem=send_sem.at[tick, way],
-            recv_sem=recv_sem.at[tick, block, half],
+            recv_sem=recv_sem.at[tick, block, tree],
             device_id={"blk": around[way]},
             device_id_type=pl.DeviceIdType.MESH,
         )
 
-    def send(tick, block, pair):
-        for half in range(2):
-            tree = pair * 2 + half
-            for way in range(4):
-                @pl.when(sends[tick][tree][way])
-                def _():
-                    chunk_copy(tick, block, half, way).start()
-
-    def receive(tick, block, pair):
-        for half in range(2):
-            tree = pair * 2 + half
-            chunk_copy(tick, block, half, 0).wait_recv()
-            for way in range(4):
-                @pl.when(sends[tick][tree][way])
-                def _():
-                    chunk_copy(tick, block, half, way).start()
+    def send(tick, block, tree):
+        for way in range(4):
+            @pl.when(places[tick][0][tree][way])
+            def _():
+                chunk_copy(tick, block, tree, way).start()
+
+    def forward(tick, slot):
+        for tree in range(4):
+            index = slot - places[tick][1][tree]
+
+            @pl.when((me != tick) & (index >= 0) & (index < number(tick)))
+            def _():
+                block = tick + 1 + index
+                chunk_copy(tick, block, tree, 0).wait_recv()
+                send(tick, block, tree)
 
     def wait_load(block):
         pltpu.make_async_copy(front.at[pl.ds(0, BLOCK)], rows.at[block], load_sem.at[block]).wait()
 
     def store(block):
-        return pltpu.make_async_copy(rows.at[block], out.at[block], store_sem.at[block])
+        for half in range(2):
+            part = block * 2 + half
+            if isinstance(block, int) and block < TICKS:
+                start = block * WIDTH + half * HALF
+            else:
+                start = jnp.where(
+                    part < 16, 4096 + part * HALF, jnp.where(part < 20, (part - 16) * WIDTH + P_SIZE, part * HALF - 768)
+                )
+                start = pl.multiple_of(start, HALF)
+            pltpu.make_async_copy(
+                rows.at[block, pl.ds(half * HALF, HALF)], out.at[pl.ds(start, HALF)], store_sem.at[block]
+            ).start()
 
     def invert(tick):
         matrix = rows[tick, :, :P_SIZE]
@@ -159,84 +193,93 @@
         urows[:, :P_SIZE] = (rows[tick, :, :P_SIZE] * keep).astype(BF16)
         urows[:, P_SIZE:] = rows[tick, :, P_SIZE:].astype(BF16)
 
-    def paired(first, body):
-        body(first, 0)
-        count = BLOCKS - 1 - first
-
+    def loop(first, last, body):
         def step(index, carry):
-            body(first + 1 + 2 * index, 1)
-            body(first + 2 + 2 * index, 0)
+            body(index)
             return carry
 
-        lax.fori_loop(0, count // 2, step, 0)
-        if count % 2:
-            body(BLOCKS - 1, 1)
+        lax.fori_loop(first, last, step, 0)
 
     wait_load(0)
-    store(0).start()
+    store(0)
 
     @pl.when(me == 0)
     def _():
         invert(0)
 
-        def own(block, pair):
+        def own(block):
             wait_load(block)
             multiply(0, block)
-            send(0, block, pair)
-
-        paired(1, own)
+            for tree in range(4):
+                send(0, block, tree)
+
+        loop(1, BLOCKS, own)
+
+    def update(tick, block, pivot=False):
+        if tick == 0:
+            @pl.when(me != 0)
+            def _():
+                wait_load(block)
+
+        rows[block] = rows[block] - dot(panel[tick, block], urows[...])
+        if pivot or tick == TICKS - 1:
+            store(block)
+        if tick + 1 < TICKS:
+            @pl.when(me == tick + 1)
+            def _():
+                if pivot:
+                    invert(tick + 1)
+                else:
+                    multiply(tick + 1, block)
+                    for tree in range(4):
+                        send(tick + 1, block, tree)
+
+    for tick in range(TICKS + 1):
+        def early(slot):
+            if tick > 0:
+                forward(tick - 1, number(tick - 1) + slot)
+            if tick < TICKS:
+                forward(tick, slot)
+            if tick > 0:
+                update(tick - 1, tick + number(tick - 1) - BEHIND + slot)
+
+        loop(0, BEHIND, early)
+        if tick < TICKS:
+            pivot_rows(tick)
+            forward(tick, BEHIND)
+            update(tick, tick + 1, pivot=tick + 1 < TICKS)
+
+            def late(slot):
+                forward(tick, slot)
+                update(tick, tick + 1 - BEHIND + slot)
+
+            loop(BEHIND + 1, number(tick), late)
 
     for tick in range(TICKS):
-        pivot_rows(tick)
-
-        def visit(block, pair):
-            @pl.when(me != tick)
-            def _():
-                receive(tick, block, pair)
-                if tick == 0:
-                    wait_load(block)
-
-            rows[block] = rows[block] - dot(panel[tick, block], urows[...])
-            if tick + 1 < TICKS:
-                is_pivot = isinstance(block, int) and block == tick + 1
-                if is_pivot:
-                    store(block).start()
-
-                @pl.when(me == tick + 1)
-                def _():
-                    if is_pivot:
-                        invert(tick + 1)
-                    else:
-                        multiply(tick + 1, block)
-                        send(tick + 1, block, 1 - pair)
-            else:
-                store(block).start()
-
-        paired(tick + 1, visit)
-
-    for tick in range(TICKS):
-        number = BLOCKS - 1 - tick
-        for pair, amount in enumerate((number - number // 2, number // 2)):
-            for way in range(4):
-                @pl.when(sends[tick][2 * pair][way] | sends[tick][2 * pair + 1][way])
-                def _():
-                    sent = panel.at[tick, pl.ds(0, amount), pl.ds(0, HALF)]
-                    pltpu.make_async_remote_copy(
-                        src_ref=sent,
-                        dst_ref=sent,
-                        send_sem=send_sem.at[tick, way],
-                        recv_sem=recv_sem.at[tick, 0, 0],
-                        device_id={"blk": around[way]},
-                        device_id_type=pl.DeviceIdType.MESH,
-                    ).wait_send()
+        for way in range(4):
+            used = places[tick][0][0][way]
+            for tree in range(1, 4):
+                used = used | places[tick][0][tree][way]
+
+            @pl.when(used)
+            def _():
+                sent = panel.at[tick, pl.ds(0, number(tick)), pl.ds(0, CHUNK)]
+                pltpu.make_async_remote_copy(
+                    src_ref=sent,
+                    dst_ref=sent,
+                    send_sem=send_sem.at[tick, way],
+                    recv_sem=recv_sem.at[tick, 0, 0],
+                    device_id={"blk": around[way]},
+                    device_id_type=pl.DeviceIdType.MESH,
+                ).wait_send()
     for block in range(BLOCKS):
-        store(block).wait()
+        pltpu.make_async_copy(rows.at[block], out.at[pl.ds(0, BLOCK)], store_sem.at[block]).wait()
 
 
 def factor(front):
     return pl.pallas_call(
         kernel,
-        out_shape=jax.ShapeDtypeStruct((BLOCKS, BLOCK, WIDTH), F32),
+        out_shape=jax.ShapeDtypeStruct(front.shape, F32),
         in_specs=[pl.BlockSpec(memory_space=pl.ANY)],
         out_specs=pl.BlockSpec(memory_space=pl.ANY),
         scratch_shapes=[
@@ -248,7 +291,7 @@
             pltpu.SemaphoreType.DMA((BLOCKS,)),
             pltpu.SemaphoreType.DMA((BLOCKS,)),
             pltpu.SemaphoreType.DMA((TICKS, 4)),
-            pltpu.SemaphoreType.DMA((TICKS, BLOCKS, 2)),
+            pltpu.SemaphoreType.DMA((TICKS, BLOCKS, 4)),
         ],
         compiler_params=pltpu.CompilerParams(
             collective_id=0, has_side_effects=True, vmem_limit_bytes=50 * 1024 * 1024
@@ -261,18 +304,9 @@
     order, width = front.shape
     member = lax.axis_index("blk")
     groups = lax.axis_size("front")
-    held = factor(front)
-    parts = []
-    for block in range(BLOCKS):
-        at = 0
-        for start, size in pieces(block):
-            parts.append((start, held[block, at : at + size]))
-            at += size
-    parts.sort(key=lambda part: part[0])
-    factored = jnp.concatenate([part[1] for part in parts], axis=0)
-
+    factored = factor(front)
     keep_left = (member >= TICKS).astype(F32)
-    tail = held[TICKS : TICKS + 3].reshape(NB * RB, width)
+    tail = factored[order - NB * RB :]
     tail = jnp.concatenate([tail[:, :P_SIZE] * keep_left, tail[:, P_SIZE:]], axis=1)
     cont = tail.astype(BF16).reshape(NB, RB, width)
     dest = parent_group.reshape(NB)

time: 1670 us -> 202 us (0.12)
  Pallas kernels: 1590 us -> 150 us
  local copies, waits for them, and re-layouts: 50.5 us -> 13.9 us
    pallas_call x1, Pallas kernels: 1590 us -> 150 us  [factor(): pl.pallas_call(kernel, out_shape=jax.ShapeDtypeStruct(front.shape, F32),...]
    unnamed x27 -> x3, local copies, waits for them, and re-layouts: 43.7 us -> 9.13 us
  transfers between devices with their start and end apart: 2 -> 2, of which waited for: 1 -> 1; matrix products, arithmetic and copies ran while one was open for 3% -> 3% of each run, Pallas kernels for 95% -> 74%
where the time goes in v2:
time: 202 us
  Pallas kernels  150 us (74%)
  waiting for transfers between devices  21.5 us (11%)
  local copies, waits for them, and re-layouts  13.9 us (7%)
  starting transfers between devices  9.87 us (5%)
  other arithmetic  4.07 us (2%)
  matrix products  2.37 us (1%)
    pallas_call x1, Pallas kernels, factor(): pl.pallas_call(kernel, out_shape=jax.ShapeDtypeStruct(front.shape, F32),...  150 us
    all_to_all x1, waiting for transfers between devices, local(): lax.all_to_all(outgoing, 'front', split_axis=0, concat_axis=0, tiled=True)  21.5 us
    unnamed x3, local copies, waits for them, and re-layouts  9.13 us
    all_to_all x1, starting transfers between devices, local(): lax.all_to_all(outgoing, 'front', split_axis=0, concat_axis=0, tiled=True)  5.4 us
    all_to_all x1, starting transfers between devices, local(): lax.all_to_all(address, 'front', split_axis=0, concat_axis=0, tiled=True)  4.47 us
  transfers between devices with their start and end apart: 2, of which 1 were waited for; matrix products, arithmetic and copies ran while one was open for 3% of the time, Pallas kernels for 74%

profile of v2, /device:TPU:4, one launch (start us, length us, event | category | flops | bytes accessed | tf_op | source)
XLA Modules:
  0.0 201.9 jit_solution(3742009981459319417)
XLA Ops:
  0.6 0.9 convert_reduce_fusion
  1.5 0.7 iota_compare_fusion.2
  2.2 0.8 convolution_convert_fusion.1
  3.1 0.6 copy.14
  3.7 4.5 %all-to-all-start = ((bf16[8,2,8]{2,1,0:T(2,128)(2,1)}), bf16[8,2,8]{2,1,0:T(2,128)(2,1)S(1)}, u32[]{:S(2)}, u32[]{:S(2)}) async-start(bf16[8,2,8]{2,1,0:T(2,128)(2,1)} %copy.14), calls=%async_computation | async-start | bytes 8192 | tf_op jit(solution)/shard_map/all_to_all | solution.py:326
  8.1 149.5 %factor.1 = f32[6144,384]{1,0:T(8,128)} custom-call(f32[6144,384]{1,0:T(8,128)} %front.1), custom_call_target="tpu_custom_call" | custom-call | tf_op jit(solution)/shard_map/factor/pallas_call | solution.py:280
  157.6 1.0 slice.15
  158.7 0.1 copy.16
  158.8 1.2 multiply_convert_fusion
  160.0 0.2 copy.15
  160.2 0.6 convolution_convert_fusion
  160.8 2.4 %copy.17 = bf16[8,2,128,384]{3,1,2,0:T(2,128)(2,1)} copy(bf16[8,2,128,384]{3,0,1,2:T(8,128)(2,1)S(1)} %convolution_convert_fusion) | data formatting | bytes 3145728 | tf_op jit(solution)/shard_map/convert_element_type | solution.py:322
  163.2 0.0 all-to-all-done
  163.2 5.4 %all-to-all-start.1 = ((bf16[8,2,128,384]{3,1,2,0:T(2,128)(2,1)}), bf16[8,2,128,384]{3,1,2,0:T(2,128)(2,1)S(1)}, u32[]{:S(2)}, u32[]{:S(2)}) async-start(bf16[8,2,128,384]{3,1,2,0:T(2,128)(2,1)} %copy.17), calls=%async_computation.1 | async-start | bytes 3145728 | tf_op jit(solution)/shard_map/all_to_all | solution.py:325
  168.6 0.1 copy.18
  168.6 21.5 %all-to-all-done.1 = bf16[8,2,128,384]{3,1,2,0:T(2,128)(2,1)S(1)} async-done(((bf16[8,2,128,384]{3,1,2,0:T(2,128)(2,1)}), bf16[8,2,128,384]{3,1,2,0:T(2,128)(2,1)S(1)}, u32[]{:S(2)}, u32[]{:S(2)}) %all-to-all-start.1) | async-done | bytes 1572896 | tf_op jit(solution)/shard_map/all_to_all | solution.py:325
  190.1 1.0 fusion.2
  191.1 0.0 copy-start
  191.1 0.3 copy.20
  191.4 1.1 copy-done
  192.5 1.3 bitcast_add_fusion
  193.8 8.0 %copy.28 = f32[6144,384]{1,0:T(8,128)} copy(f32[6144,384]{1,0:T(8,128)} %factor.1) | data formatting | bytes 18874368
  (1 shorter events, 0.0 us)
Async XLA Ops:
  3.7 159.5 %all-to-all-start = ((bf16[8,2,8]{2,1,0:T(2,128)(2,1)}), bf16[8,2,8]{2,1,0:T(2,128)(2,1)S(1)}, u32[]{:S(2)}, u32[]{:S(2)}) async-start(bf16[8,2,8]{2,1,0:T(2,128)(2,1)} %copy.14), calls=%async_computation | async-start | bytes 8192 | tf_op jit(solution)/shard_map/all_to_all | solution.py:326
  163.2 27.0 %all-to-all-start.1 = ((bf16[8,2,128,384]{3,1,2,0:T(2,128)(2,1)}), bf16[8,2,128,384]{3,1,2,0:T(2,128)(2,1)S(1)}, u32[]{:S(2)}, u32[]{:S(2)}) async-start(bf16[8,2,128,384]{3,1,2,0:T(2,128)(2,1)} %copy.17), calls=%async_computation.1 | async-start | bytes 3145728 | tf_op jit(solution)/shard_map/all_to_all | solution.py:325
  191.1 1.4 copy-start

commit v3 on v2

--- a/solution.py
+++ b/solution.py
@@ -11,13 +11,16 @@
 NB = 6
 CAP = 2
 ASM_BLOCKS = 8
+GROUPS = 8
 SIDE = 4
 WIDTH = 384
 BLOCK = 256
 HALF = BLOCK // 2
 CHUNK = BLOCK // 4
-LAG = 3
-BEHIND = 5 * LAG
+LAG = 6
+NEAR = 3 * LAG
+FAR = 5 * LAG
+TAIL = 7
 BLOCKS = 24
 F32 = jnp.float32
 BF16 = jnp.bfloat16
@@ -64,6 +67,9 @@
     return BLOCKS - 1 - tick
 
 
+FIRST_SLOT = tuple(sum(number(tick) for tick in range(last)) for last in range(TICKS))
+
+
 def split(value):
     high = value.astype(BF16)
     return high, (value - high.astype(F32)).astype(BF16)
@@ -77,8 +83,12 @@
     return dot(a[0], b[0]) + dot(a[0], b[1]) + dot(a[1], b[0])
 
 
-def kernel(front, out, rows, panel, urows, inv_high, inv_low, load_sem, store_sem, send_sem, recv_sem):
+def kernel(
+    front, dest, target, rows, arrived, tags, panel, urows, inv_high, inv_low, cont, picked, labels,
+    load_sem, send_sem, recv_sem, slot_send, slot_recv, tag_send, tag_recv,
+):
     me = lax.axis_index("blk")
+    mine = lax.axis_index("front")
     x = lax.rem(me, SIDE)
     z = lax.div(me, SIDE)
     around = [
@@ -99,7 +109,14 @@
     barrier = pltpu.get_barrier_semaphore()
     for other in around:
         pl.semaphore_signal(barrier, inc=1, device_id={"blk": other}, device_id_type=pl.DeviceIdType.MESH)
-    pl.semaphore_wait(barrier, 4)
+    for offset in range(1, GROUPS):
+        pl.semaphore_signal(
+            barrier,
+            inc=1,
+            device_id={"front": lax.rem(mine + offset, GROUPS)},
+            device_id_type=pl.DeviceIdType.MESH,
+        )
+    pl.semaphore_wait(barrier, 4 + GROUPS - 1)
 
     def place(tick):
         dx = lax.rem(x - tick % SIDE + SIDE, SIDE)
@@ -120,7 +137,9 @@
             for node, depth in DEPTH.items():
                 lag = jnp.where(turned[tree] == node, depth * LAG, lag)
             lags.append(lag)
-        return result, lags
+        deepest = jnp.maximum(jnp.maximum(lags[0], lags[1]), jnp.maximum(lags[2], lags[3]))
+        deepest = jnp.maximum(deepest, NEAR)
+        return result, lags, deepest
 
     places = [place(tick) for tick in range(TICKS)]
 
@@ -153,20 +172,6 @@
 
     def wait_load(block):
         pltpu.make_async_copy(front.at[pl.ds(0, BLOCK)], rows.at[block], load_sem.at[block]).wait()
-
-    def store(block):
-        for half in range(2):
-            part = block * 2 + half
-            if isinstance(block, int) and block < TICKS:
-                start = block * WIDTH + half * HALF
-            else:
-                start = jnp.where(
-                    part < 16, 4096 + part * HALF, jnp.where(part < 20, (part - 16) * WIDTH + P_SIZE, part * HALF - 768)
-                )
-                start = pl.multiple_of(start, HALF)
-            pltpu.make_async_copy(
-                rows.at[block, pl.ds(half * HALF, HALF)], out.at[pl.ds(start, HALF)], store_sem.at[block]
-            ).start()
 
     def invert(tick):
         matrix = rows[tick, :, :P_SIZE]
@@ -190,8 +195,8 @@
 
     def pivot_rows(tick):
         keep = jnp.where(me > tick, 1.0, 0.0).astype(F32)
-        urows[:, :P_SIZE] = (rows[tick, :, :P_SIZE] * keep).astype(BF16)
-        urows[:, P_SIZE:] = rows[tick, :, P_SIZE:].astype(BF16)
+        urows[tick, :, :P_SIZE] = (rows[tick, :, :P_SIZE] * keep).astype(BF16)
+        urows[tick, :, P_SIZE:] = rows[tick, :, P_SIZE:].astype(BF16)
 
     def loop(first, last, body):
         def step(index, carry):
@@ -201,7 +206,6 @@
         lax.fori_loop(first, last, step, 0)
 
     wait_load(0)
-    store(0)
 
     @pl.when(me == 0)
     def _():
@@ -215,46 +219,112 @@
 
         loop(1, BLOCKS, own)
 
-    def update(tick, block, pivot=False):
-        if tick == 0:
-            @pl.when(me != 0)
-            def _():
-                wait_load(block)
-
-        rows[block] = rows[block] - dot(panel[tick, block], urows[...])
-        if pivot or tick == TICKS - 1:
-            store(block)
-        if tick + 1 < TICKS:
-            @pl.when(me == tick + 1)
-            def _():
-                if pivot:
-                    invert(tick + 1)
-                else:
-                    multiply(tick + 1, block)
-                    for tree in range(4):
-                        send(tick + 1, block, tree)
-
-    for tick in range(TICKS + 1):
-        def early(slot):
-            if tick > 0:
-                forward(tick - 1, number(tick - 1) + slot)
-            if tick < TICKS:
-                forward(tick, slot)
-            if tick > 0:
-                update(tick - 1, tick + number(tick - 1) - BEHIND + slot)
-
-        loop(0, BEHIND, early)
-        if tick < TICKS:
-            pivot_rows(tick)
-            forward(tick, BEHIND)
-            update(tick, tick + 1, pivot=tick + 1 < TICKS)
-
-            def late(slot):
-                forward(tick, slot)
-                update(tick, tick + 1 - BEHIND + slot)
-
-            loop(BEHIND + 1, number(tick), late)
-
+    def slot_copy(offset):
+        peer = lax.rem(mine + offset, GROUPS)
+        return pltpu.make_async_remote_copy(
+            src_ref=picked.at[peer],
+            dst_ref=arrived.at[mine],
+            send_sem=slot_send.at[offset],
+            recv_sem=slot_recv.at[offset],
+            device_id={"front": peer},
+            device_id_type=pl.DeviceIdType.MESH,
+        )
+
+    def tag_copy(offset):
+        peer = lax.rem(mine + offset, GROUPS)
+        return pltpu.make_async_remote_copy(
+            src_ref=labels.at[peer],
+            dst_ref=tags.at[mine],
+            send_sem=tag_send.at[offset],
+            recv_sem=tag_recv.at[offset],
+            device_id={"front": peer},
+            device_id_type=pl.DeviceIdType.MESH,
+        )
+
+    slots = []
+    for block in range(NB):
+        slot = jnp.int32(0)
+        for before in range(block):
+            slot = slot + jnp.where(dest[before] == dest[block], 1, 0)
+        slots.append(slot)
+    lane = lax.broadcasted_iota(jnp.int32, (1, 128), 1)
+    for group in range(GROUPS):
+        label = jnp.full((1, 128), -1, jnp.int32)
+        for block in range(NB):
+            label = jnp.where(lane == jnp.where(dest[block] == group, slots[block], -1), target[block], label)
+        labels[group] = label
+    tags[mine] = labels[mine]
+    for offset in range(1, GROUPS):
+        tag_copy(offset).start()
+
+    def exchange():
+        keep = jnp.where(me >= TICKS, 1.0, 0.0).astype(F32)
+        for block in range(NB):
+            part = pl.ds(block % 2 * RB, RB)
+            cont[block, :, :P_SIZE] = (rows[TICKS + block // 2, part, :P_SIZE] * keep).astype(BF16)
+            cont[block, :, P_SIZE:] = rows[TICKS + block // 2, part, P_SIZE:].astype(BF16)
+        cont[NB] = jnp.zeros((RB, WIDTH), BF16)
+        for group in range(GROUPS):
+            for slot in range(CAP):
+                number_of = jnp.int32(NB)
+                for block in range(NB):
+                    number_of = jnp.where((dest[block] == group) & (slots[block] == slot), block, number_of)
+                picked[group, slot] = cont[number_of]
+        for offset in (4, 3, 5, 2, 6, 1, 7):
+            slot_copy(offset).start()
+        arrived[mine] = picked[mine]
+
+    def update(tick, index, first):
+        @pl.when((index >= 0) & (index < number(tick)))
+        def _():
+            block = tick + 1 + index
+            if first:
+                @pl.when(index == 0)
+                def _():
+                    pivot_rows(tick)
+
+            if tick == 0:
+                @pl.when(me != 0)
+                def _():
+                    wait_load(block)
+
+            rows[block] = rows[block] - dot(panel[tick, block], urows[tick])
+            if tick + 1 < TICKS:
+                @pl.when(me == tick + 1)
+                def _():
+                    if first:
+                        @pl.when(index == 0)
+                        def _():
+                            invert(tick + 1)
+
+                    @pl.when(index > 0)
+                    def _():
+                        multiply(tick + 1, block)
+                        for tree in range(4):
+                            send(tick + 1, block, tree)
+            elif first:
+                @pl.when(block == TAIL)
+                def _():
+                    exchange()
+
+    ends = [FIRST_SLOT[tick] + number(tick) + FAR for tick in range(TICKS)]
+    starts = [FIRST_SLOT[tick] + NEAR for tick in range(TICKS)]
+    firsts = [FIRST_SLOT[tick] + FAR + 3 for tick in range(TICKS)]
+    marks = sorted(set(list(FIRST_SLOT) + ends + starts + firsts))
+    for begin, end in zip(marks[:-1], marks[1:]):
+        def step(slot):
+            for tick in range(TICKS):
+                if FIRST_SLOT[tick] <= begin < ends[tick]:
+                    forward(tick, slot - FIRST_SLOT[tick])
+            for tick in range(TICKS):
+                if starts[tick] <= begin < ends[tick]:
+                    update(tick, slot - FIRST_SLOT[tick] - places[tick][2], begin < firsts[tick])
+
+        loop(begin, end, step)
+
+    for offset in range(1, GROUPS):
+        slot_copy(offset).wait()
+        tag_copy(offset).wait()
     for tick in range(TICKS):
         for way in range(4):
             used = places[tick][0][0][way]
@@ -272,62 +342,105 @@
                     device_id={"blk": around[way]},
                     device_id_type=pl.DeviceIdType.MESH,
                 ).wait_send()
-    for block in range(BLOCKS):
-        pltpu.make_async_copy(rows.at[block], out.at[pl.ds(0, BLOCK)], store_sem.at[block]).wait()
-
-
-def factor(front):
+
+
+def factor(front, dest, target):
     return pl.pallas_call(
         kernel,
-        out_shape=jax.ShapeDtypeStruct(front.shape, F32),
-        in_specs=[pl.BlockSpec(memory_space=pl.ANY)],
-        out_specs=pl.BlockSpec(memory_space=pl.ANY),
+        out_shape=(
+            pltpu.VMEM((BLOCKS, BLOCK, WIDTH), F32),
+            pltpu.VMEM((GROUPS, CAP, RB, WIDTH), BF16),
+            jax.ShapeDtypeStruct((GROUPS, 1, 128), jnp.int32),
+        ),
+        in_specs=[
+            pl.BlockSpec(memory_space=pl.ANY),
+            pl.BlockSpec(memory_space=pltpu.SMEM),
+            pl.BlockSpec(memory_space=pltpu.SMEM),
+        ],
+        out_specs=(
+            pl.BlockSpec(memory_space=pltpu.VMEM),
+            pl.BlockSpec(memory_space=pltpu.VMEM),
+            pl.BlockSpec(memory_space=pltpu.VMEM),
+        ),
         scratch_shapes=[
-            pltpu.VMEM((BLOCKS, BLOCK, WIDTH), F32),
             pltpu.VMEM((TICKS, BLOCKS, BLOCK, P_SIZE), BF16),
-            pltpu.VMEM((P_SIZE, WIDTH), BF16),
+            pltpu.VMEM((TICKS, P_SIZE, WIDTH), BF16),
             pltpu.VMEM((P_SIZE, P_SIZE), BF16),
             pltpu.VMEM((P_SIZE, P_SIZE), BF16),
-            pltpu.SemaphoreType.DMA((BLOCKS,)),
+            pltpu.VMEM((NB + 1, RB, WIDTH), BF16),
+            pltpu.VMEM((GROUPS, CAP, RB, WIDTH), BF16),
+            pltpu.VMEM((GROUPS, 1, 128), jnp.int32),
             pltpu.SemaphoreType.DMA((BLOCKS,)),
             pltpu.SemaphoreType.DMA((TICKS, 4)),
             pltpu.SemaphoreType.DMA((TICKS, BLOCKS, 4)),
+            pltpu.SemaphoreType.DMA((GROUPS,)),
+            pltpu.SemaphoreType.DMA((GROUPS,)),
+            pltpu.SemaphoreType.DMA((GROUPS,)),
+            pltpu.SemaphoreType.DMA((GROUPS,)),
         ],
         compiler_params=pltpu.CompilerParams(
-            collective_id=0, has_side_effects=True, vmem_limit_bytes=50 * 1024 * 1024
+            collective_id=0, has_side_effects=True, vmem_limit_bytes=45 * 1024 * 1024
         ),
         name="factor",
-    )(front)
+    )(front, dest, target)
+
+
+def finish_kernel(rows, arrived, tags, base, factored, assembled, total, rows_sem, base_sem, out_sem):
+    load = pltpu.make_async_copy(base, total, base_sem)
+    load.start()
+    copies = []
+    for block in range(BLOCKS):
+        at = 0
+        for start, size in pieces(block):
+            copies.append(
+                pltpu.make_async_copy(
+                    rows.at[block, pl.ds(at, size)], factored.at[pl.ds(start, size)], rows_sem.at[len(copies)]
+                )
+            )
+            copies[-1].start()
+            at += size
+    load.wait()
+    for group in range(GROUPS):
+        for slot in range(CAP):
+            place = tags[group, 0, slot]
+
+            @pl.when(place >= 0)
+            def _():
+                part = pl.ds(pl.multiple_of(place * RB, RB), RB)
+                total[part] = total[part] + arrived[group, slot].astype(F32)
+
+    store = pltpu.make_async_copy(total, assembled, out_sem)
+    store.start()
+    for copy in copies:
+        copy.wait()
+    store.wait()
+
+
+def finish(rows, arrived, tags, base, shape):
+    return pl.pallas_call(
+        finish_kernel,
+        out_shape=(jax.ShapeDtypeStruct(shape, F32), jax.ShapeDtypeStruct(base.shape, F32)),
+        in_specs=[
+            pl.BlockSpec(memory_space=pltpu.VMEM),
+            pl.BlockSpec(memory_space=pltpu.VMEM),
+            pl.BlockSpec(memory_space=pltpu.SMEM),
+            pl.BlockSpec(memory_space=pl.ANY),
+        ],
+        out_specs=(pl.BlockSpec(memory_space=pl.ANY), pl.BlockSpec(memory_space=pl.ANY)),
+        scratch_shapes=[
+            pltpu.VMEM((ASM_BLOCKS * RB, WIDTH), F32),
+            pltpu.SemaphoreType.DMA((BLOCKS + 2,)),
+            pltpu.SemaphoreType.DMA,
+            pltpu.SemaphoreType.DMA,
+        ],
+        compiler_params=pltpu.CompilerParams(vmem_limit_bytes=16 * 1024 * 1024),
+        name="finish",
+    )(rows, arrived, tags, base)
 
 
 def local(front, parent_group, row_block, parent_base):
-    order, width = front.shape
-    member = lax.axis_index("blk")
-    groups = lax.axis_size("front")
-    factored = factor(front)
-    keep_left = (member >= TICKS).astype(F32)
-    tail = factored[order - NB * RB :]
-    tail = jnp.concatenate([tail[:, :P_SIZE] * keep_left, tail[:, P_SIZE:]], axis=1)
-    cont = tail.astype(BF16).reshape(NB, RB, width)
-    dest = parent_group.reshape(NB)
-    target_block = row_block.reshape(NB)
-    offset_hot = (target_block[:, None] == jnp.arange(ASM_BLOCKS, dtype=jnp.int32)[None, :]).astype(BF16)
-    number = jnp.arange(NB)
-    earlier = (dest[None, :] == dest[:, None]) & (number[None, :] < number[:, None])
-    slot = jnp.sum(earlier.astype(jnp.int32), axis=1)
-    pick = (dest[None, None, :] == jnp.arange(groups, dtype=jnp.int32)[:, None, None]) & (
-        slot[None, None, :] == jnp.arange(CAP, dtype=jnp.int32)[None, :, None]
-    )
-    pick = pick.astype(BF16)
-    outgoing = jnp.einsum("gci,irk->gcrk", pick, cont, preferred_element_type=F32).astype(BF16)
-    address = jnp.einsum("gci,ia->gca", pick, offset_hot, preferred_element_type=F32).astype(BF16)
-    incoming, received_address = (
-        lax.all_to_all(outgoing, "front", split_axis=0, concat_axis=0, tiled=True),
-        lax.all_to_all(address, "front", split_axis=0, concat_axis=0, tiled=True),
-    )
-    added = jnp.einsum("gca,gcrk->ark", received_address, incoming, preferred_element_type=F32)
-    assembled = parent_base + added.reshape(ASM_BLOCKS * RB, width)
-    return (factored, assembled)
+    rows, arrived, tags = factor(front, parent_group.reshape(NB), row_block.reshape(NB))
+    return finish(rows, arrived, tags, parent_base, front.shape)
 
 
 def solution(mesh):

time: 202 us -> 137 us (0.68)
  waiting for transfers between devices: 21.5 us -> 0 us
  Pallas kernels: 150 us -> 135 us
  local copies, waits for them, and re-layouts: 13.9 us -> 0.68 us
  starting transfers between devices: 9.87 us -> 0 us
  other arithmetic: 4.07 us -> 0 us
  matrix products: 2.37 us -> 0 us
    all_to_all x2 -> x0, waiting for transfers between devices: 21.5 us -> none  [the longest x1 21.5 us: local(): lax.all_to_all(outgoing, 'front', split_axis=0, concat_axis=0, tiled=True)]
    pallas_call x1 -> x2, Pallas kernels: 150 us -> 135 us  [the longest x1 130 us: factor(): pl.pallas_call(kernel, out_shape=(pltpu.VMEM((BLOCKS, BLOCK, WIDTH), F32)...]
    all_to_all x2 -> x0, starting transfers between devices: 9.87 us -> none  [the longest x1 5.4 us: local(): lax.all_to_all(outgoing, 'front', split_axis=0, concat_axis=0, tiled=True)]
    unnamed x3 -> x4, local copies, waits for them, and re-layouts: 9.13 us -> 0.68 us
    convert_element_type x2 -> x0, local copies, waits for them, and re-layouts: 2.95 us -> none  [the longest x1 2.36 us: local(): jnp.einsum('gci,irk->gcrk', pick, cont, preferred_element_type=F32)]
    dot_general x3 -> x0, matrix products: 2.37 us -> none  [the longest x1 0.97 us: local(): jnp.einsum('gca,gcrk->ark', received_address, incoming, preferred_element...]
  transfers between devices with their start and end apart: 2 -> 0, of which waited for: 1 -> 0; matrix products, arithmetic and copies ran while one was open for 3% -> 0% of each run, Pallas kernels for 74% -> 0%
where the time goes in v3:
time: 137 us
  Pallas kernels  135 us (99%)
    pallas_call x1, Pallas kernels, factor(): pl.pallas_call(kernel, out_shape=(pltpu.VMEM((BLOCKS, BLOCK, WIDTH), F32)...  130 us
    pallas_call x1, Pallas kernels, finish(): pl.pallas_call(finish_kernel, out_shape=(jax.ShapeDtypeStruct(shape, F32)...  5.05 us

profile of v3, /device:TPU:4, one launch (start us, length us, event | category | flops | bytes accessed | tf_op | source)
XLA Modules:
  0.0 136.6 jit_solution(15124048498919790528)
XLA Ops:
  0.6 0.0 copy-start
  0.6 130.0 %factor.1 = (f32[24,256,384]{2,1,0:T(8,128)S(1)}, bf16[8,2,128,384]{3,2,1,0:T(8,128)(2,1)S(1)}, s32[8,1,128]{2,1,0:T(1,128)}) custom-call(f32[6144,384]{1,0:T(8,128)} %front.1, s32[6]{0:T(128)} %bitcast.2, s32[6]{0:T(128)} %bitcast.3), custom_call_target="tpu_custom_call" | custom-call | tf_op jit(solution)/shard_map/factor/pallas_call | solution.py:348
  130.7 0.0 copy-done
  130.7 0.0 copy-start.1
  130.7 0.7 copy-done.1
  131.4 5.0 %finish.1 = (f32[6144,384]{1,0:T(8,128)}, f32[1024,384]{1,0:T(8,128)}) custom-call(f32[24,256,384]{2,1,0:T(8,128)S(1)} %get-tuple-element.5.rows, bf16[8,2,128,384]{3,2,1,0:T(8,128)(2,1)S(1)} %get-tuple-element.6.arrived, s32[8,1,128]{2,1,0:T(1,128)S(1)} %copy-done.1, f32[1024,384]{1,0:T(8,128)S(1)} %copy-done), custom_call_target="tpu_custom_call" | custom-call | tf_op jit(solution)/shard_map/finish/pallas_call | solution.py:420
Async XLA Ops:
  0.6 130.0 %copy-start = (f32[1024,384]{1,0:T(8,128)S(1)}, f32[1024,384]{1,0:T(8,128)}, u32[]{:S(2)}) copy-start(f32[1024,384]{1,0:T(8,128)} %base.1) | copy-start | bytes 4718596
  130.7 0.7 copy-start.1

commit v4 on v3

--- a/solution.py
+++ b/solution.py
@@ -17,9 +17,10 @@
 BLOCK = 256
 HALF = BLOCK // 2
 CHUNK = BLOCK // 4
-LAG = 6
-NEAR = 3 * LAG
-FAR = 5 * LAG
+LAGS = (0, 4, 10, 16, 22, 28)
+FIRST_SLOT = (0, 17, 34, 53, 78)
+LEAST = 13
+UPDATES = tuple(max(LEAST, LAGS[depth]) for depth in (0, 3, 4, 5))
 TAIL = 7
 BLOCKS = 24
 F32 = jnp.float32
@@ -65,9 +66,6 @@
 
 def number(tick):
     return BLOCKS - 1 - tick
-
-
-FIRST_SLOT = tuple(sum(number(tick) for tick in range(last)) for last in range(TICKS))
 
 
 def split(value):
@@ -98,14 +96,6 @@
         lax.rem(z + SIDE - 1, SIDE) * SIDE + x,
     ]
 
-    for block in range(BLOCKS):
-        at = 0
-        for start, size in pieces(block):
-            pltpu.make_async_copy(
-                front.at[pl.ds(start, size)], rows.at[block, pl.ds(at, size)], load_sem.at[block]
-            ).start()
-            at += size
-
     barrier = pltpu.get_barrier_semaphore()
     for other in around:
         pl.semaphore_signal(barrier, inc=1, device_id={"blk": other}, device_id_type=pl.DeviceIdType.MESH)
@@ -116,7 +106,16 @@
             device_id={"front": lax.rem(mine + offset, GROUPS)},
             device_id_type=pl.DeviceIdType.MESH,
         )
-    pl.semaphore_wait(barrier, 4 + GROUPS - 1)
+
+    def load(block):
+        at = 0
+        for start, size in pieces(block):
+            pltpu.make_async_copy(
+                front.at[pl.ds(start, size)], rows.at[block, pl.ds(at, size)], load_sem.at[block]
+            ).start()
+            at += size
+
+    load(0)
 
     def place(tick):
         dx = lax.rem(x - tick % SIDE + SIDE, SIDE)
@@ -135,10 +134,10 @@
             result.append(ways)
             lag = jnp.int32(0)
             for node, depth in DEPTH.items():
-                lag = jnp.where(turned[tree] == node, depth * LAG, lag)
+                lag = jnp.where(turned[tree] == node, LAGS[depth], lag)
             lags.append(lag)
         deepest = jnp.maximum(jnp.maximum(lags[0], lags[1]), jnp.maximum(lags[2], lags[3]))
-        deepest = jnp.maximum(deepest, NEAR)
+        deepest = jnp.maximum(deepest, LEAST)
         return result, lags, deepest
 
     places = [place(tick) for tick in range(TICKS)]
@@ -206,11 +205,17 @@
         lax.fori_loop(first, last, step, 0)
 
     wait_load(0)
+    for block in range(1, BLOCKS):
+        load(block)
 
     @pl.when(me == 0)
     def _():
         invert(0)
 
+    pl.semaphore_wait(barrier, 4 + GROUPS - 1)
+
+    @pl.when(me == 0)
+    def _():
         def own(block):
             wait_load(block)
             multiply(0, block)
@@ -307,17 +312,17 @@
                 def _():
                     exchange()
 
-    ends = [FIRST_SLOT[tick] + number(tick) + FAR for tick in range(TICKS)]
-    starts = [FIRST_SLOT[tick] + NEAR for tick in range(TICKS)]
-    firsts = [FIRST_SLOT[tick] + FAR + 3 for tick in range(TICKS)]
-    marks = sorted(set(list(FIRST_SLOT) + ends + starts + firsts))
+    moves = [(FIRST_SLOT[tick] + LAGS[1], FIRST_SLOT[tick] + number(tick) + LAGS[5]) for tick in range(TICKS)]
+    works = [(FIRST_SLOT[tick] + min(UPDATES), FIRST_SLOT[tick] + number(tick) + max(UPDATES)) for tick in range(TICKS)]
+    firsts = [FIRST_SLOT[tick] + max(UPDATES) + 3 for tick in range(TICKS)]
+    marks = sorted({mark for pair in moves + works for mark in pair} | set(firsts))
     for begin, end in zip(marks[:-1], marks[1:]):
         def step(slot):
             for tick in range(TICKS):
-                if FIRST_SLOT[tick] <= begin < ends[tick]:
+                if moves[tick][0] <= begin < moves[tick][1]:
                     forward(tick, slot - FIRST_SLOT[tick])
             for tick in range(TICKS):
-                if starts[tick] <= begin < ends[tick]:
+                if works[tick][0] <= begin < works[tick][1]:
                     update(tick, slot - FIRST_SLOT[tick] - places[tick][2], begin < firsts[tick])
 
         loop(begin, end, step)
@@ -350,7 +355,7 @@
         out_shape=(
             pltpu.VMEM((BLOCKS, BLOCK, WIDTH), F32),
             pltpu.VMEM((GROUPS, CAP, RB, WIDTH), BF16),
-            jax.ShapeDtypeStruct((GROUPS, 1, 128), jnp.int32),
+            pltpu.VMEM((GROUPS, 1, 128), jnp.int32),
         ),
         in_specs=[
             pl.BlockSpec(memory_space=pl.ANY),
@@ -385,7 +390,11 @@
     )(front, dest, target)
 
 
-def finish_kernel(rows, arrived, tags, base, factored, assembled, total, rows_sem, base_sem, out_sem):
+def finish_kernel(
+    rows, arrived, tags, base, factored, assembled, labels, tags_sem, total, rows_sem, base_sem, out_sem
+):
+    read = pltpu.make_async_copy(tags, labels, tags_sem)
+    read.start()
     load = pltpu.make_async_copy(base, total, base_sem)
     load.start()
     copies = []
@@ -400,9 +409,10 @@
             copies[-1].start()
             at += size
     load.wait()
+    read.wait()
     for group in range(GROUPS):
         for slot in range(CAP):
-            place = tags[group, 0, slot]
+            place = labels[group, 0, slot]
 
             @pl.when(place >= 0)
             def _():
@@ -423,11 +433,13 @@
         in_specs=[
             pl.BlockSpec(memory_space=pltpu.VMEM),
             pl.BlockSpec(memory_space=pltpu.VMEM),
-            pl.BlockSpec(memory_space=pltpu.SMEM),
+            pl.BlockSpec(memory_space=pltpu.VMEM),
             pl.BlockSpec(memory_space=pl.ANY),
         ],
         out_specs=(pl.BlockSpec(memory_space=pl.ANY), pl.BlockSpec(memory_space=pl.ANY)),
         scratch_shapes=[
+            pltpu.SMEM((GROUPS, 1, 128), jnp.int32),
+            pltpu.SemaphoreType.DMA,
             pltpu.VMEM((ASM_BLOCKS * RB, WIDTH), F32),
             pltpu.SemaphoreType.DMA((BLOCKS + 2,)),
             pltpu.SemaphoreType.DMA,

time: 137 us -> 130 us (0.949)
  Pallas kernels: 135 us -> 129 us
    pallas_call x1, Pallas kernels: 130 us -> 125 us  [factor(): pl.pallas_call(kernel, out_shape=(pltpu.VMEM((BLOCKS, BLOCK, WIDTH), F32)...]
where the time goes in v4:
time: 130 us
  Pallas kernels  129 us (99%)
    pallas_call x1, Pallas kernels, factor(): pl.pallas_call(kernel, out_shape=(pltpu.VMEM((BLOCKS, BLOCK, WIDTH), F32)...  125 us
    pallas_call x1, Pallas kernels, finish(): pl.pallas_call(finish_kernel, out_shape=(jax.ShapeDtypeStruct(shape, F32)...  4.46 us

profile of v4, /device:TPU:4, one launch (start us, length us, event | category | flops | bytes accessed | tf_op | source)
XLA Modules:
  0.0 130.2 jit_solution(3562669387446665671)
XLA Ops:
  0.6 0.0 copy-start
  0.6 124.9 %factor.1 = (f32[24,256,384]{2,1,0:T(8,128)S(1)}, bf16[8,2,128,384]{3,2,1,0:T(8,128)(2,1)S(1)}, s32[8,1,128]{2,1,0:T(1,128)S(1)}) custom-call(f32[6144,384]{1,0:T(8,128)} %front.1, s32[6]{0:T(128)} %bitcast.2, s32[6]{0:T(128)} %bitcast.3), custom_call_target="tpu_custom_call" | custom-call | tf_op jit(solution)/shard_map/factor/pallas_call | solution.py:353
  125.5 0.0 copy-done
  125.6 4.5 %finish.1 = (f32[6144,384]{1,0:T(8,128)}, f32[1024,384]{1,0:T(8,128)}) custom-call(f32[24,256,384]{2,1,0:T(8,128)S(1)} %get-tuple-element.5.rows, bf16[8,2,128,384]{3,2,1,0:T(8,128)(2,1)S(1)} %get-tuple-element.6.arrived, s32[8,1,128]{2,1,0:T(1,128)S(1)} %get-tuple-element.7.tags, f32[1024,384]{1,0:T(8,128)S(1)} %copy-done), custom_call_target="tpu_custom_call" | custom-call | tf_op jit(solution)/shard_map/finish/pallas_call | solution.py:430
Async XLA Ops:
  0.6 124.9 %copy-start = (f32[1024,384]{1,0:T(8,128)S(1)}, f32[1024,384]{1,0:T(8,128)}, u32[]{:S(2)}) copy-start(f32[1024,384]{1,0:T(8,128)} %base.1) | copy-start | bytes 4718596

commit v5 on v4

--- a/solution.py
+++ b/solution.py
@@ -17,10 +17,17 @@
 BLOCK = 256
 HALF = BLOCK // 2
 CHUNK = BLOCK // 4
-LAGS = (0, 4, 10, 16, 22, 28)
-FIRST_SLOT = (0, 17, 34, 53, 78)
-LEAST = 13
-UPDATES = tuple(max(LEAST, LAGS[depth]) for depth in (0, 3, 4, 5))
+LAGS = (
+    (0, 2, 8, 13, 22, 28),
+    (0, 5, 6, 15, 20, 26),
+    (0, 2, 9, 16, 21, 34),
+    (0, 1, 8, 12, 15, 30),
+    (0, 1, 4, 12, 13, 19),
+)
+FIRST_SLOT = (0, 28, 43, 66, 85)
+LEAST = (22, 3, 10, 15, 3)
+IDLE = 1000
+UPDATES = tuple(tuple(max(LEAST[tick], LAGS[tick][depth]) for depth in (0, 3, 4, 5)) for tick in range(TICKS))
 TAIL = 7
 BLOCKS = 24
 F32 = jnp.float32
@@ -77,12 +84,18 @@
     return jnp.dot(a, b, preferred_element_type=F32)
 
 
-def dot3(a, b):
-    return dot(a[0], b[0]) + dot(a[0], b[1]) + dot(a[1], b[0])
+def left(value):
+    high, low = split(value)
+    return jnp.concatenate([high, high, low], axis=1)
+
+
+def right(value):
+    high, low = split(value)
+    return jnp.concatenate([high, low, high], axis=0)
 
 
 def kernel(
-    front, dest, target, rows, arrived, tags, panel, urows, inv_high, inv_low, cont, picked, labels,
+    front, dest, target, rows, arrived, tags, panel, urows, inverse, cont, picked, labels,
     load_sem, send_sem, recv_sem, slot_send, slot_recv, tag_send, tag_recv,
 ):
     me = lax.axis_index("blk")
@@ -132,12 +145,12 @@
                     has = has | (turned[tree] == node)
                 ways.append(has)
             result.append(ways)
-            lag = jnp.int32(0)
+            lag = jnp.int32(IDLE)
             for node, depth in DEPTH.items():
-                lag = jnp.where(turned[tree] == node, LAGS[depth], lag)
+                lag = jnp.where(turned[tree] == node, LAGS[tick][depth], lag)
             lags.append(lag)
         deepest = jnp.maximum(jnp.maximum(lags[0], lags[1]), jnp.maximum(lags[2], lags[3]))
-        deepest = jnp.maximum(deepest, LEAST)
+        deepest = jnp.where(me == tick, LEAST[tick], jnp.maximum(deepest, LEAST[tick]))
         return result, lags, deepest
 
     places = [place(tick) for tick in range(TICKS)]
@@ -163,7 +176,7 @@
         for tree in range(4):
             index = slot - places[tick][1][tree]
 
-            @pl.when((me != tick) & (index >= 0) & (index < number(tick)))
+            @pl.when((index >= 0) & (index < number(tick)))
             def _():
                 block = tick + 1 + index
                 chunk_copy(tick, block, tree, 0).wait_recv()
@@ -180,15 +193,14 @@
         on_diagonal = jnp.where(eye, matrix, 0.0)
         by_row = 1.0 / jnp.sum(on_diagonal, axis=1, keepdims=True)
         by_column = 1.0 / jnp.sum(on_diagonal, axis=0, keepdims=True)
-        first = jnp.where(eye, 2.0 * by_row, 0.0) - by_row * matrix * by_column
-        first = split(first)
-        residual = jnp.where(eye, 2.0, 0.0) - dot3(split(matrix), first)
-        high, low = split(dot3(first, split(residual)))
-        inv_high[...] = high
-        inv_low[...] = low
+        once = jnp.where(eye, 0.0, matrix * by_column)
+        side = left(once)
+        twice = dot(side, right(once))
+        thrice = dot(side, right(twice))
+        inverse[...] = right(by_row * (jnp.where(eye, 1.0, 0.0) - once + twice - thrice))
 
     def multiply(tick, block):
-        mult = dot3(split(rows[block, :, :P_SIZE]), (inv_high[...], inv_low[...]))
+        mult = dot(left(rows[block, :, :P_SIZE]), inverse[...])
         rows[block, :, :P_SIZE] = mult
         panel[tick, block] = mult.astype(BF16)
 
@@ -312,9 +324,9 @@
                 def _():
                     exchange()
 
-    moves = [(FIRST_SLOT[tick] + LAGS[1], FIRST_SLOT[tick] + number(tick) + LAGS[5]) for tick in range(TICKS)]
-    works = [(FIRST_SLOT[tick] + min(UPDATES), FIRST_SLOT[tick] + number(tick) + max(UPDATES)) for tick in range(TICKS)]
-    firsts = [FIRST_SLOT[tick] + max(UPDATES) + 3 for tick in range(TICKS)]
+    moves = [(FIRST_SLOT[tick] + LAGS[tick][1], FIRST_SLOT[tick] + number(tick) + LAGS[tick][5]) for tick in range(TICKS)]
+    works = [(FIRST_SLOT[tick] + min(UPDATES[tick]), FIRST_SLOT[tick] + number(tick) + max(UPDATES[tick])) for tick in range(TICKS)]
+    firsts = [FIRST_SLOT[tick] + max(UPDATES[tick]) + 3 for tick in range(TICKS)]
     marks = sorted({mark for pair in moves + works for mark in pair} | set(firsts))
     for begin, end in zip(marks[:-1], marks[1:]):
         def step(slot):
@@ -370,8 +382,7 @@
         scratch_shapes=[
             pltpu.VMEM((TICKS, BLOCKS, BLOCK, P_SIZE), BF16),
             pltpu.VMEM((TICKS, P_SIZE, WIDTH), BF16),
-            pltpu.VMEM((P_SIZE, P_SIZE), BF16),
-            pltpu.VMEM((P_SIZE, P_SIZE), BF16),
+            pltpu.VMEM((3 * P_SIZE, P_SIZE), BF16),
             pltpu.VMEM((NB + 1, RB, WIDTH), BF16),
             pltpu.VMEM((GROUPS, CAP, RB, WIDTH), BF16),
             pltpu.VMEM((GROUPS, 1, 128), jnp.int32),

time: 130 us -> 129 us (level)
  no operation moved by 1% of the time
where the time goes in v5:
time: 129 us
  Pallas kernels  128 us (99%)
    pallas_call x1, Pallas kernels, factor(): pl.pallas_call(kernel, out_shape=(pltpu.VMEM((BLOCKS, BLOCK, WIDTH), F32)...  124 us
    pallas_call x1, Pallas kernels, finish(): pl.pallas_call(finish_kernel, out_shape=(jax.ShapeDtypeStruct(shape, F32)...  4.46 us

profile of v5, /device:TPU:4, one launch (start us, length us, event | category | flops | bytes accessed | tf_op | source)
XLA Modules:
  0.0 129.1 jit_solution(8316014971729976121)
XLA Ops:
  0.6 0.0 copy-start
  0.6 123.9 %factor.1 = (f32[24,256,384]{2,1,0:T(8,128)S(1)}, bf16[8,2,128,384]{3,2,1,0:T(8,128)(2,1)S(1)}, s32[8,1,128]{2,1,0:T(1,128)S(1)}) custom-call(f32[6144,384]{1,0:T(8,128)} %front.1, s32[6]{0:T(128)} %bitcast.2, s32[6]{0:T(128)} %bitcast.3), custom_call_target="tpu_custom_call" | custom-call | tf_op jit(solution)/shard_map/factor/pallas_call | solution.py:365
  124.5 0.0 copy-done
  124.5 4.5 %finish.1 = (f32[6144,384]{1,0:T(8,128)}, f32[1024,384]{1,0:T(8,128)}) custom-call(f32[24,256,384]{2,1,0:T(8,128)S(1)} %get-tuple-element.5.rows, bf16[8,2,128,384]{3,2,1,0:T(8,128)(2,1)S(1)} %get-tuple-element.6.arrived, s32[8,1,128]{2,1,0:T(1,128)S(1)} %get-tuple-element.7.tags, f32[1024,384]{1,0:T(8,128)S(1)} %copy-done), custom_call_target="tpu_custom_call" | custom-call | tf_op jit(solution)/shard_map/finish/pallas_call | solution.py:441
Async XLA Ops:
  0.6 123.9 %copy-start = (f32[1024,384]{1,0:T(8,128)S(1)}, f32[1024,384]{1,0:T(8,128)}, u32[]{:S(2)}) copy-start(f32[1024,384]{1,0:T(8,128)} %base.1) | copy-start | bytes 4718596

commit v6 on v5

--- a/solution.py
+++ b/solution.py
@@ -236,6 +236,8 @@
 
         loop(1, BLOCKS, own)
 
+    pivot_rows(0)
+
     def slot_copy(offset):
         peer = lax.rem(mine + offset, GROUPS)
         return pltpu.make_async_remote_copy(
@@ -281,25 +283,21 @@
             cont[block, :, :P_SIZE] = (rows[TICKS + block // 2, part, :P_SIZE] * keep).astype(BF16)
             cont[block, :, P_SIZE:] = rows[TICKS + block // 2, part, P_SIZE:].astype(BF16)
         cont[NB] = jnp.zeros((RB, WIDTH), BF16)
-        for group in range(GROUPS):
+        for offset in (4, 3, 5, 2, 6, 1, 7, 0):
+            group = lax.rem(mine + offset, GROUPS)
             for slot in range(CAP):
                 number_of = jnp.int32(NB)
                 for block in range(NB):
                     number_of = jnp.where((dest[block] == group) & (slots[block] == slot), block, number_of)
                 picked[group, slot] = cont[number_of]
-        for offset in (4, 3, 5, 2, 6, 1, 7):
-            slot_copy(offset).start()
+            if offset:
+                slot_copy(offset).start()
         arrived[mine] = picked[mine]
 
     def update(tick, index, first):
         @pl.when((index >= 0) & (index < number(tick)))
         def _():
             block = tick + 1 + index
-            if first:
-                @pl.when(index == 0)
-                def _():
-                    pivot_rows(tick)
-
             if tick == 0:
                 @pl.when(me != 0)
                 def _():
@@ -319,6 +317,12 @@
                         multiply(tick + 1, block)
                         for tree in range(4):
                             send(tick + 1, block, tree)
+
+                if first:
+                    @pl.when(index == 0)
+                    def _():
+                        pivot_rows(tick + 1)
+
             elif first:
                 @pl.when(block == TAIL)
                 def _():

time: 129 us -> 129 us (level)
  no operation moved by 1% of the time
where the time goes in v6:
time: 129 us
  Pallas kernels  128 us (99%)
    pallas_call x1, Pallas kernels, factor(): pl.pallas_call(kernel, out_shape=(pltpu.VMEM((BLOCKS, BLOCK, WIDTH), F32)...  124 us
    pallas_call x1, Pallas kernels, finish(): pl.pallas_call(finish_kernel, out_shape=(jax.ShapeDtypeStruct(shape, F32)...  4.46 us

profile of v6, /device:TPU:4, one launch (start us, length us, event | category | flops | bytes accessed | tf_op | source)
XLA Modules:
  0.0 129.3 jit_solution(9001749746481654198)
XLA Ops:
  0.6 0.0 copy-start
  0.6 124.0 %factor.1 = (f32[24,256,384]{2,1,0:T(8,128)S(1)}, bf16[8,2,128,384]{3,2,1,0:T(8,128)(2,1)S(1)}, s32[8,1,128]{2,1,0:T(1,128)S(1)}) custom-call(f32[6144,384]{1,0:T(8,128)} %front.1, s32[6]{0:T(128)} %bitcast.2, s32[6]{0:T(128)} %bitcast.3), custom_call_target="tpu_custom_call" | custom-call | tf_op jit(solution)/shard_map/factor/pallas_call | solution.py:369
  124.6 0.0 copy-done
  124.6 4.5 %finish.1 = (f32[6144,384]{1,0:T(8,128)}, f32[1024,384]{1,0:T(8,128)}) custom-call(f32[24,256,384]{2,1,0:T(8,128)S(1)} %get-tuple-element.5.rows, bf16[8,2,128,384]{3,2,1,0:T(8,128)(2,1)S(1)} %get-tuple-element.6.arrived, s32[8,1,128]{2,1,0:T(1,128)S(1)} %get-tuple-element.7.tags, f32[1024,384]{1,0:T(8,128)S(1)} %copy-done), custom_call_target="tpu_custom_call" | custom-call | tf_op jit(solution)/shard_map/finish/pallas_call | solution.py:445
Async XLA Ops:
  0.6 124.0 %copy-start = (f32[1024,384]{1,0:T(8,128)S(1)}, f32[1024,384]{1,0:T(8,128)}, u32[]{:S(2)}) copy-start(f32[1024,384]{1,0:T(8,128)} %base.1) | copy-start | bytes 4718596
